TPU v7x, 128 devices: a whole 4x4x4 slice. The times are simulated.
128 devices in a mesh: grp: 4 (over y), own: 32 (over x, z, core).
Axes of the slice: x: 4, y: 4, z: 4, core: 2. Of those that a mesh axis runs over, the one named last changes fastest.
Arguments:
- embeddings: float32 [98304, 768], P(('grp', 'own')), may hold values from -64 to 64
- cluster_ids: int32 [98304], P(('grp', 'own')), may hold values from 0 to 511, as said below
- owner_map: int32 [512], replicated, may hold values from 0 to 31, as said below
- source_order: int32 [98304], P(('grp', 'own')), may hold values from 0 to 767, as said below
Outputs:
- dup_score: float32 [98304], P(('grp', 'own'))
- centroids: float32 [512, 768], P('own')
Inputs may be any that keep to these rules, and one draw needn't show every extreme that they name: `owner_map`: every owner index is given to exactly 16 clusters. `cluster_ids`: within the 768 rows of one device, at most 48 rows have clusters of one owner index; in every draw some owner index receives exactly 48 rows from every device, and every device sends exactly 48 rows to some owner index. Cluster sizes are uneven and some clusters may be empty. `source_order`: each aligned block of 768 entries is a permutation of 0 to 767.
All inputs are finite; a program needn't handle non-finite values.
Results may differ from a plain program's by a relative error of at most 0.0003.
Values sent between devices are 32-bit elements; how exact they have to be, the bound alone decides.
A program may use at most 128 MiB of HBM per device.

v0:
```python
import jax
import jax.numpy as jnp
from jax import lax
from jax.sharding import PartitionSpec as P

CL_OWN = 16
sharpness = 6.0


def unit_rows(embeddings):
    squares = jnp.sum(embeddings * embeddings, axis=1, keepdims=True)
    return embeddings * lax.rsqrt(squares + 1e-06)


def owner_positions(owner_map):
    cluster_index = jnp.arange(owner_map.shape[0], dtype=jnp.int32)
    same_owner = owner_map[:, None] == owner_map[None, :]
    earlier = cluster_index[None, :] < cluster_index[:, None]
    before = jnp.sum((same_owner & earlier).astype(jnp.int32), axis=1)
    return owner_map * CL_OWN + before


def masked_weights(left_rows, left_ids, right_rows, right_ids):
    scores = jnp.einsum(
        "id,jd->ij",
        left_rows,
        right_rows,
        preferred_element_type=jnp.float32,
        precision=lax.Precision.HIGHEST,
    )
    linked = (left_ids[:, None] == right_ids[None, :]) & (left_ids[:, None] >= 0)
    return jnp.where(linked, jnp.exp(sharpness * (scores - 1.0)), 0.0)


def tile_sums(left_rows, left_ids, right_rows, right_ids):
    right_count = right_rows.shape[0]
    block_rows = 512
    block_count = right_count // block_rows
    right_blocks = right_rows.reshape(block_count, block_rows, right_rows.shape[1])
    id_blocks = right_ids.reshape(block_count, block_rows)

    def one_block(row_total, block_pair):
        weights = masked_weights(left_rows, left_ids, block_pair[0], block_pair[1])
        column_part = None
        return (row_total + jnp.sum(weights, axis=1), column_part)

    row_sums, column_sums = lax.scan(
        one_block, jnp.zeros((left_rows.shape[0],), jnp.float32), (right_blocks, id_blocks)
    )
    return (row_sums, column_sums)


def local(embeddings, cluster_ids, owner_map, source_order):
    row_count, feature_width = embeddings.shape
    owner_count = lax.axis_size("own")
    capacity = 2 * row_count // owner_count
    slot_count = owner_count * capacity
    cluster_count = owner_map.shape[0]
    unit_embed = unit_rows(embeddings)
    cluster_index = jnp.arange(cluster_count, dtype=jnp.int32)
    cluster_match = cluster_ids[:, None] == cluster_index[None, :]
    row_owner = jnp.sum(jnp.where(cluster_match, owner_map[None, :], 0), axis=1)
    owner_hot = (row_owner[:, None] == jnp.arange(owner_count, dtype=jnp.int32)[None, :]).astype(
        jnp.int32
    )
    rank_index = jnp.sum(jnp.cumsum(owner_hot, axis=0) * owner_hot, axis=1) - 1
    slot_index = row_owner * capacity + rank_index
    send_rows = jnp.zeros((slot_count, feature_width), jnp.float32).at[slot_index].set(unit_embed)
    send_ids = jnp.full((slot_count,), -1, jnp.int32).at[slot_index].set(cluster_ids)
    held_rows, held_ids = (
        lax.all_to_all(
            send_rows.reshape(owner_count, capacity, feature_width),
            "own",
            split_axis=0,
            concat_axis=0,
            tiled=True,
        ),
        lax.all_to_all(
            send_ids.reshape(owner_count, capacity), "own", split_axis=0, concat_axis=0, tiled=True
        ),
    )
    held_rows = held_rows.reshape(slot_count, feature_width)
    held_ids = held_ids.reshape(slot_count)
    row_sums, column_sums = tile_sums(
        held_rows,
        held_ids,
        lax.all_gather(held_rows, "grp", axis=0, tiled=True),
        lax.all_gather(held_ids, "grp", axis=0, tiled=True),
    )
    returned = lax.all_to_all(
        row_sums.reshape(owner_count, capacity), "own", split_axis=0, concat_axis=0, tiled=True
    )
    row_score = jnp.log(returned.reshape(slot_count)[slot_index])
    dup_score = jnp.zeros((row_count,), jnp.float32).at[source_order].set(row_score)
    position = owner_positions(owner_map)
    position_index = jnp.arange(cluster_count, dtype=jnp.int32)
    ordered = jnp.sum(
        jnp.where(position[None, :] == position_index[:, None], cluster_index[None, :], 0), axis=1
    )
    cluster_hot = (cluster_ids[:, None] == ordered[None, :]).astype(jnp.float32)
    cluster_terms = lax.dot_general(
        cluster_hot,
        unit_embed,
        (((0,), (0,)), ((), ())),
        preferred_element_type=jnp.float32,
        precision=lax.Precision.HIGHEST,
    )
    partial_value = lax.psum_scatter(cluster_terms, "own", scatter_dimension=0, tiled=True)
    cluster_sums = lax.psum(partial_value, "grp")
    centroids = cluster_sums * lax.rsqrt(
        jnp.mean(cluster_sums * cluster_sums, axis=1, keepdims=True) + 1e-06
    )
    return (dup_score, centroids)


def solution(mesh):
    placed = (P(("grp", "own"), None), P(("grp", "own")), P(), P(("grp", "own")))
    return jax.shard_map(
        local,
        mesh=mesh,
        in_specs=placed,
        out_specs=(P(("grp", "own")), P("own", None)),
        check_vma=False,
    )
```

profile of v0, /device:TPU:1, one launch (start us, length us, event | category | flops | bytes accessed | tf_op | source)
XLA Modules:
  0.0 433.6 jit_solution(5770465693371880921)
XLA Ops:
  13.3 9.7 %scatter_custom_fusion.1 = f32[1536,768]{1,0:T(8,128)} fusion(s32[768]{0:T(1024)S(1)} %fusion.26, f32[]{:T(128)} %constant.55.clone.1, f32[768,768]{1,0:T(8,128)S(1)} %copy-done, f32[768]{0:T(1024)S(1)} %add_rsqrt_fusion), kind=kCustom, calls=%fused_computation.17 | custom fusion | flops 589824 | bytes 7081988 | tf_op jit(solution)/shard_map/scatter | solution.py:68
  23.1 9.6 %all-to-all-start.1 = ((f32[32,48,768]{2,1,0:T(8,128)}), f32[32,48,768]{2,1,0:T(8,128)}, u32[]{:S(2)}, u32[]{:S(2)}) async-start(f32[32,48,768]{2,1,0:T(8,128)} %bitcast.46), calls=%async_computation.1 | async-start | bytes 9437184 | tf_op jit(solution)/shard_map/all_to_all | solution.py:71
  37.1 55.2 %all-to-all-done.1 = f32[32,48,768]{2,1,0:T(8,128)} async-done(((f32[32,48,768]{2,1,0:T(8,128)}), f32[32,48,768]{2,1,0:T(8,128)}, u32[]{:S(2)}, u32[]{:S(2)}) %all-to-all-start.1) | async-done | bytes 4718624 | tf_op jit(solution)/shard_map/all_to_all | solution.py:71
  96.4 9.8 %all-to-all-start = ((s32[32,1,48]{2,1,0:T(1,128)}), s32[32,1,48]{2,1,0:T(1,128)S(1)}, u32[]{:S(2)}, u32[]{:S(2)}) async-start(s32[32,1,48]{2,1,0:T(1,128)} %all_to_all.17), calls=%async_computation | async-start | bytes 32768 | tf_op jit(solution)/shard_map/all_to_all | solution.py:78
  106.2 6.8 %all-to-all-done = s32[32,1,48]{2,1,0:T(1,128)S(1)} async-done(((s32[32,1,48]{2,1,0:T(1,128)}), s32[32,1,48]{2,1,0:T(1,128)S(1)}, u32[]{:S(2)}, u32[]{:S(2)}) %all-to-all-start) | async-done | bytes 6176 | tf_op jit(solution)/shard_map/all_to_all | solution.py:78
  114.4 10.7 %all-gather = s32[4,1,1536]{2,1,0:T(1,128)S(1)} all-gather(s32[1,1,1536]{2,1,0:T(1,128)S(1)} %reshape.149), channel_id=1, replica_groups=mesh['grp'=4,'own'=32] {'grp'}, dimensions={0}, use_global_device_ids=true | all-gather | bytes 30720 | tf_op jit(solution)/shard_map/all_gather | solution.py:88
  125.1 16.3 %psum.7 = f32[16,768]{1,0:T(8,128)S(1)} all-reduce(f32[16,768]{1,0:T(8,128)} %reduce-scatter.2.cloned.1.call-done), channel_id=1, replica_groups=mesh['grp'=4,'own'=32] {'grp'}, use_global_device_ids=true, to_apply=%region_14.15 | all-reduce | flops 12288 | bytes 98304 | tf_op jit(solution)/shard_map/psum | solution.py:109
  141.6 127.8 %all-gather.3.cloned.1.call-done = f32[6144,768]{1,0:T(8,128)} async-done(((f32[1536,768]{1,0:T(8,128)}), f32[6144,768]{1,0:T(8,128)}) %all-gather.3.cloned.1.call-update) | async-done | bytes 18874384 | tf_op jit(solution)/shard_map/all_gather | solution.py:87
  269.4 131.6 %while.14 = (s32[]{:T(128)}, f32[1536]{0:T(1024)S(1)}, s32[32,48]{1,0:T(8,128)}, s32[12,512]{1,0:T(8,128)S(1)}, f32[12,512,768]{2,1,0:T(8,128)}, /*index=5*/f32[...) while((s32[]{:T(128)}, f32[1536]{0:T(1024)S(1)}, s32[32,48]{1,0:T(8,128)}, ...), condition=%wide.wide.region_9.10_spmd.clone, body=%wide.wide.region_7.9_spmd.clone.sunk | while | flops 7252478976 | bytes 6338155 | solution.py:47
  269.4 10.9 %fusion.38 = f32[1536]{0:T(1024)S(1)} fusion(f32[1536,768]{1,0:T(8,128)} %get-tuple-element.203, f32[12,512,768]{2,1,0:T(8,128)} %get-tuple-element.202, s32[]{:T(128)} %get-tuple-element.189, pred[1536]{0:T(1024)(128)(4,1)S(1)} %broadcast_compare_fusion.3, s32[512]{0:T(512)S(1)} %bitcast.50, s32[1536]{0:T(1024)S(1)} %get-tuple-element.204), kind=kOutput, calls=%fused_computation.11.clone.clone.1 | convolution fusion | flops 7252474368 | bytes 6307840 | tf_op jit(solution)/shard_map/while/body/eval_jaxpr/id,jd->ij/dot_general | solution.py:24
  280.4 10.9 %fusion.38 = f32[1536]{0:T(1024)S(1)} fusion(f32[1536,768]{1,0:T(8,128)} %get-tuple-element.203, f32[12,512,768]{2,1,0:T(8,128)} %get-tuple-element.202, s32[]{:T(128)} %get-tuple-element.189, pred[1536]{0:T(1024)(128)(4,1)S(1)} %broadcast_compare_fusion.3, s32[512]{0:T(512)S(1)} %bitcast.50, s32[1536]{0:T(1024)S(1)} %get-tuple-element.204), kind=kOutput, calls=%fused_computation.11.clone.clone.1 | convolution fusion | flops 7252474368 | bytes 6307840 | tf_op jit(solution)/shard_map/while/body/eval_jaxpr/id,jd->ij/dot_general | solution.py:24
  291.4 10.9 %fusion.38 = f32[1536]{0:T(1024)S(1)} fusion(f32[1536,768]{1,0:T(8,128)} %get-tuple-element.203, f32[12,512,768]{2,1,0:T(8,128)} %get-tuple-element.202, s32[]{:T(128)} %get-tuple-element.189, pred[1536]{0:T(1024)(128)(4,1)S(1)} %broadcast_compare_fusion.3, s32[512]{0:T(512)S(1)} %bitcast.50, s32[1536]{0:T(1024)S(1)} %get-tuple-element.204), kind=kOutput, calls=%fused_computation.11.clone.clone.1 | convolution fusion | flops 7252474368 | bytes 6307840 | tf_op jit(solution)/shard_map/while/body/eval_jaxpr/id,jd->ij/dot_general | solution.py:24
  302.3 10.9 %fusion.38 = f32[1536]{0:T(1024)S(1)} fusion(f32[1536,768]{1,0:T(8,128)} %get-tuple-element.203, f32[12,512,768]{2,1,0:T(8,128)} %get-tuple-element.202, s32[]{:T(128)} %get-tuple-element.189, pred[1536]{0:T(1024)(128)(4,1)S(1)} %broadcast_compare_fusion.3, s32[512]{0:T(512)S(1)} %bitcast.50, s32[1536]{0:T(1024)S(1)} %get-tuple-element.204), kind=kOutput, calls=%fused_computation.11.clone.clone.1 | convolution fusion | flops 7252474368 | bytes 6307840 | tf_op jit(solution)/shard_map/while/body/eval_jaxpr/id,jd->ij/dot_general | solution.py:24
  313.3 10.9 %fusion.38 = f32[1536]{0:T(1024)S(1)} fusion(f32[1536,768]{1,0:T(8,128)} %get-tuple-element.203, f32[12,512,768]{2,1,0:T(8,128)} %get-tuple-element.202, s32[]{:T(128)} %get-tuple-element.189, pred[1536]{0:T(1024)(128)(4,1)S(1)} %broadcast_compare_fusion.3, s32[512]{0:T(512)S(1)} %bitcast.50, s32[1536]{0:T(1024)S(1)} %get-tuple-element.204), kind=kOutput, calls=%fused_computation.11.clone.clone.1 | convolution fusion | flops 7252474368 | bytes 6307840 | tf_op jit(solution)/shard_map/while/body/eval_jaxpr/id,jd->ij/dot_general | solution.py:24
  324.3 10.9 %fusion.38 = f32[1536]{0:T(1024)S(1)} fusion(f32[1536,768]{1,0:T(8,128)} %get-tuple-element.203, f32[12,512,768]{2,1,0:T(8,128)} %get-tuple-element.202, s32[]{:T(128)} %get-tuple-element.189, pred[1536]{0:T(1024)(128)(4,1)S(1)} %broadcast_compare_fusion.3, s32[512]{0:T(512)S(1)} %bitcast.50, s32[1536]{0:T(1024)S(1)} %get-tuple-element.204), kind=kOutput, calls=%fused_computation.11.clone.clone.1 | convolution fusion | flops 7252474368 | bytes 6307840 | tf_op jit(solution)/shard_map/while/body/eval_jaxpr/id,jd->ij/dot_general | solution.py:24
  335.3 10.9 %fusion.38 = f32[1536]{0:T(1024)S(1)} fusion(f32[1536,768]{1,0:T(8,128)} %get-tuple-element.203, f32[12,512,768]{2,1,0:T(8,128)} %get-tuple-element.202, s32[]{:T(128)} %get-tuple-element.189, pred[1536]{0:T(1024)(128)(4,1)S(1)} %broadcast_compare_fusion.3, s32[512]{0:T(512)S(1)} %bitcast.50, s32[1536]{0:T(1024)S(1)} %get-tuple-element.204), kind=kOutput, calls=%fused_computation.11.clone.clone.1 | convolution fusion | flops 7252474368 | bytes 6307840 | tf_op jit(solution)/shard_map/while/body/eval_jaxpr/id,jd->ij/dot_general | solution.py:24
  346.2 10.9 %fusion.38 = f32[1536]{0:T(1024)S(1)} fusion(f32[1536,768]{1,0:T(8,128)} %get-tuple-element.203, f32[12,512,768]{2,1,0:T(8,128)} %get-tuple-element.202, s32[]{:T(128)} %get-tuple-element.189, pred[1536]{0:T(1024)(128)(4,1)S(1)} %broadcast_compare_fusion.3, s32[512]{0:T(512)S(1)} %bitcast.50, s32[1536]{0:T(1024)S(1)} %get-tuple-element.204), kind=kOutput, calls=%fused_computation.11.clone.clone.1 | convolution fusion | flops 7252474368 | bytes 6307840 | tf_op jit(solution)/shard_map/while/body/eval_jaxpr/id,jd->ij/dot_general | solution.py:24
  357.2 10.9 %fusion.38 = f32[1536]{0:T(1024)S(1)} fusion(f32[1536,768]{1,0:T(8,128)} %get-tuple-element.203, f32[12,512,768]{2,1,0:T(8,128)} %get-tuple-element.202, s32[]{:T(128)} %get-tuple-element.189, pred[1536]{0:T(1024)(128)(4,1)S(1)} %broadcast_compare_fusion.3, s32[512]{0:T(512)S(1)} %bitcast.50, s32[1536]{0:T(1024)S(1)} %get-tuple-element.204), kind=kOutput, calls=%fused_computation.11.clone.clone.1 | convolution fusion | flops 7252474368 | bytes 6307840 | tf_op jit(solution)/shard_map/while/body/eval_jaxpr/id,jd->ij/dot_general | solution.py:24
  368.2 10.9 %fusion.38 = f32[1536]{0:T(1024)S(1)} fusion(f32[1536,768]{1,0:T(8,128)} %get-tuple-element.203, f32[12,512,768]{2,1,0:T(8,128)} %get-tuple-element.202, s32[]{:T(128)} %get-tuple-element.189, pred[1536]{0:T(1024)(128)(4,1)S(1)} %broadcast_compare_fusion.3, s32[512]{0:T(512)S(1)} %bitcast.50, s32[1536]{0:T(1024)S(1)} %get-tuple-element.204), kind=kOutput, calls=%fused_computation.11.clone.clone.1 | convolution fusion | flops 7252474368 | bytes 6307840 | tf_op jit(solution)/shard_map/while/body/eval_jaxpr/id,jd->ij/dot_general | solution.py:24
  379.1 10.9 %fusion.38 = f32[1536]{0:T(1024)S(1)} fusion(f32[1536,768]{1,0:T(8,128)} %get-tuple-element.203, f32[12,512,768]{2,1,0:T(8,128)} %get-tuple-element.202, s32[]{:T(128)} %get-tuple-element.189, pred[1536]{0:T(1024)(128)(4,1)S(1)} %broadcast_compare_fusion.3, s32[512]{0:T(512)S(1)} %bitcast.50, s32[1536]{0:T(1024)S(1)} %get-tuple-element.204), kind=kOutput, calls=%fused_computation.11.clone.clone.1 | convolution fusion | flops 7252474368 | bytes 6307840 | tf_op jit(solution)/shard_map/while/body/eval_jaxpr/id,jd->ij/dot_general | solution.py:24
  390.1 10.9 %fusion.38 = f32[1536]{0:T(1024)S(1)} fusion(f32[1536,768]{1,0:T(8,128)} %get-tuple-element.203, f32[12,512,768]{2,1,0:T(8,128)} %get-tuple-element.202, s32[]{:T(128)} %get-tuple-element.189, pred[1536]{0:T(1024)(128)(4,1)S(1)} %broadcast_compare_fusion.3, s32[512]{0:T(512)S(1)} %bitcast.50, s32[1536]{0:T(1024)S(1)} %get-tuple-element.204), kind=kOutput, calls=%fused_computation.11.clone.clone.1 | convolution fusion | flops 7252474368 | bytes 6307840 | tf_op jit(solution)/shard_map/while/body/eval_jaxpr/id,jd->ij/dot_general | solution.py:24
  401.7 7.7 %all-to-all-start.2 = ((f32[32,1,48]{2,1,0:T(1,128)}), f32[32,1,48]{2,1,0:T(1,128)S(1)}, u32[]{:S(2)}, u32[]{:S(2)}) async-start(f32[32,1,48]{2,1,0:T(1,128)} %all_to_all.21), calls=%async_computation.2 | async-start | bytes 32768 | tf_op jit(solution)/shard_map/all_to_all | solution.py:90
  410.2 6.2 %all-to-all-done.2 = f32[32,1,48]{2,1,0:T(1,128)S(1)} async-done(((f32[32,1,48]{2,1,0:T(1,128)}), f32[32,1,48]{2,1,0:T(1,128)S(1)}, u32[]{:S(2)}, u32[]{:S(2)}) %all-to-all-start.2) | async-done | bytes 6176 | tf_op jit(solution)/shard_map/all_to_all | solution.py:90
  417.7 4.5 %gather_fusion = f32[768]{0:T(1024)S(1)} fusion(f32[1536]{0:T(1024)S(1)} %reshape.115, s32[1024]{0:T(1024)S(1)} %pad_clamp_fusion), kind=kCustom, calls=%fused_computation | custom fusion | bytes 9216 | tf_op jit(solution)/shard_map/gather | solution.py:93
  (85 shorter events, 22.1 us)
Async XLA Ops:
  8.0 5.3 %copy-start = (f32[768,768]{1,0:T(8,128)S(1)}, f32[768,768]{1,0:T(8,128)}, u32[]{:S(2)}) copy-start(f32[768,768]{1,0:T(8,128)} %param.6) | copy-start | bytes 7077892
  23.1 9.7 %copy-start.2 = (s32[512]{0:T(512)S(1)}, s32[512]{0:T(512)}, u32[]{:S(2)}) copy-start(s32[512]{0:T(512)} %param.8) | copy-start | bytes 6148
  23.1 10.1 %copy-start.3 = (s32[768]{0:T(1024)S(1)}, s32[768]{0:T(1024)}, u32[]{:S(2)}) copy-start(s32[768]{0:T(1024)} %param.7) | copy-start | bytes 9220
  23.1 69.2 %all-to-all-start.1 = ((f32[32,48,768]{2,1,0:T(8,128)}), f32[32,48,768]{2,1,0:T(8,128)}, u32[]{:S(2)}, u32[]{:S(2)}) async-start(f32[32,48,768]{2,1,0:T(8,128)} %bitcast.46), calls=%async_computation.1 | async-start | bytes 9437184 | tf_op jit(solution)/shard_map/all_to_all | solution.py:71
  32.7 92.4 %reduce-scatter.2.cloned.1.call-start = ((), (), s32[]{:S(2)}) async-start(), calls=%async_computation.5 | async-start | bytes 1622016 | tf_op jit(solution)/shard_map/reduce_scatter | solution.py:108
  37.0 232.4 %all-gather.3.cloned.1.call-start = ((), (), s32[]{:S(2)}) async-start(), calls=%async_computation.4 | async-start | bytes 23592960 | tf_op jit(solution)/shard_map/all_gather | solution.py:87
  92.3 13.9 %copy-start.4 = (s32[768]{0:T(1024)S(1)}, s32[768]{0:T(1024)}, u32[]{:S(2)}) copy-start(s32[768]{0:T(1024)} %param.9) | copy-start | bytes 9220
  96.4 16.6 %all-to-all-start = ((s32[32,1,48]{2,1,0:T(1,128)}), s32[32,1,48]{2,1,0:T(1,128)S(1)}, u32[]{:S(2)}, u32[]{:S(2)}) async-start(s32[32,1,48]{2,1,0:T(1,128)} %all_to_all.17), calls=%async_computation | async-start | bytes 32768 | tf_op jit(solution)/shard_map/all_to_all | solution.py:78
  113.1 156.3 %copy-start.1 = (s32[32,1,48]{2,1,0:T(1,128)}, s32[32,1,48]{2,1,0:T(1,128)S(1)}, u32[]{:S(2)}) copy-start(s32[32,1,48]{2,1,0:T(1,128)S(1)} %all-to-all-done) | copy-start | bytes 18436
  401.7 14.7 %all-to-all-start.2 = ((f32[32,1,48]{2,1,0:T(1,128)}), f32[32,1,48]{2,1,0:T(1,128)S(1)}, u32[]{:S(2)}, u32[]{:S(2)}) async-start(f32[32,1,48]{2,1,0:T(1,128)} %all_to_all.21), calls=%async_computation.2 | async-start | bytes 32768 | tf_op jit(solution)/shard_map/all_to_all | solution.py:90
Sparse Core Ops, SparseCore 0:
  37.1 80.2 reduce-scatter.1
Sparse Core Ops, SparseCore 1:
  92.4 176.9 all-gather.2
where the time goes:
time: 434 us
  waiting for transfers between devices  196 us (45%)
  matrix products  135 us (31%)
  starting transfers between devices  27.2 us (6%)
  blocking collectives  27 us (6%)
  other arithmetic  17.5 us (4%)
  between operations  15.7 us (4%)
  local copies, waits for them, and re-layouts  14.8 us (3%)
    dot_general x12, matrix products, masked_weights(): jnp.einsum('id,jd->ij', left_rows, right_rows, preferred_element_type=jnp...  131 us
    all_gather x1, waiting for transfers between devices, local(): lax.all_gather(held_rows, 'grp', axis=0, tiled=True)  128 us
    all_to_all x1, waiting for transfers between devices, local(): lax.all_to_all(send_rows.reshape(owner_count, capacity, feature_width), '...  55.2 us
    psum x1, blocking collectives, local(): cluster_sums = lax.psum(partial_value, 'grp')  16.3 us
    all_gather x1, blocking collectives, local(): lax.all_gather(held_ids, 'grp', axis=0, tiled=True)  10.7 us
    all_to_all x1, starting transfers between devices, local(): lax.all_to_all(send_ids.reshape(owner_count, capacity), 'own', split_axis...  9.77 us
    scatter x1, other arithmetic, local(): jnp.zeros((slot_count, feature_width), jnp.float32).at[slot_index]  9.72 us
    all_to_all x1, starting transfers between devices, local(): lax.all_to_all(send_rows.reshape(owner_count, capacity, feature_width), '...  9.61 us
  transfers between devices with their start and end apart: 5, of which 4 were waited for; matrix products, arithmetic and copies ran while one was open for 2% of the time, Pallas kernels for 0%

commit v1 on v0

--- a/solution.py
+++ b/solution.py
@@ -5,6 +5,15 @@
 
 CL_OWN = 16
 sharpness = 6.0
+
+
+def add_in_pairs(value, axis):
+    devices = lax.axis_size(axis)
+    total, far = (value, 1)
+    while far < devices:
+        total = total + lax.ppermute(total, axis, [(i, i ^ far) for i in range(devices)])
+        far = 2 * far
+    return total
 
 
 def unit_rows(embeddings):
@@ -106,7 +115,7 @@
         precision=lax.Precision.HIGHEST,
     )
     partial_value = lax.psum_scatter(cluster_terms, "own", scatter_dimension=0, tiled=True)
-    cluster_sums = lax.psum(partial_value, "grp")
+    cluster_sums = add_in_pairs(partial_value, "grp")
     centroids = cluster_sums * lax.rsqrt(
         jnp.mean(cluster_sums * cluster_sums, axis=1, keepdims=True) + 1e-06
     )

time: 434 us -> 434 us (level)
  blocking collectives: 27 us -> 10.4 us
  waiting for transfers between devices: 196 us -> 208 us
    psum x1 -> x0, blocking collectives: 16.3 us -> none  [local(): cluster_sums = lax.psum(partial_value, 'grp')]
    reduce_scatter x1, waiting for transfers between devices: 0.02 us -> 11.3 us  [local(): lax.psum_scatter(cluster_terms, 'own', scatter_dimension=0, tiled=True)]
    all_to_all x1, waiting for transfers between devices: 6.82 us -> 0.01 us  [local(): lax.all_to_all(send_ids.reshape(owner_count, capacity), 'own', split_axis...]
  transfers between devices with their start and end apart: 5 -> 7, of which waited for: 4 -> 5; matrix products, arithmetic and copies ran while one was open for 2% -> 2% of each run, Pallas kernels for 0% -> 0%
where the time goes in v1:
time: 434 us
  waiting for transfers between devices  208 us (48%)
  matrix products  135 us (31%)
  starting transfers between devices  31.2 us (7%)
  other arithmetic  18.3 us (4%)
  between operations  15.7 us (4%)
  local copies, waits for them, and re-layouts  14.9 us (3%)
  blocking collectives  10.4 us (2%)
    all_gather x1, waiting for transfers between devices, local(): lax.all_gather(held_rows, 'grp', axis=0, tiled=True)  132 us
    dot_general x12, matrix products, masked_weights(): jnp.einsum('id,jd->ij', left_rows, right_rows, preferred_element_type=jnp...  131 us
    all_to_all x1, waiting for transfers between devices, local(): lax.all_to_all(send_rows.reshape(owner_count, capacity, feature_width), '...  55.2 us
    reduce_scatter x1, waiting for transfers between devices, local(): lax.psum_scatter(cluster_terms, 'own', scatter_dimension=0, tiled=True)  11.3 us
    all_gather x1, blocking collectives, local(): lax.all_gather(held_ids, 'grp', axis=0, tiled=True)  10.4 us
    all_to_all x1, starting transfers between devices, local(): lax.all_to_all(send_ids.reshape(owner_count, capacity), 'own', split_axis...  9.77 us
    scatter x1, other arithmetic, local(): jnp.zeros((slot_count, feature_width), jnp.float32).at[slot_index]  9.72 us
    all_to_all x1, starting transfers between devices, local(): lax.all_to_all(send_rows.reshape(owner_count, capacity, feature_width), '...  9.61 us
  transfers between devices with their start and end apart: 7, of which 5 were waited for; matrix products, arithmetic and copies ran while one was open for 2% of the time, Pallas kernels for 0%

profile of v1, /device:TPU:1, one launch (start us, length us, event | category | flops | bytes accessed | tf_op | source)
XLA Modules:
  0.0 433.7 jit_solution(16509298002678625688)
XLA Ops:
  13.3 9.7 %scatter_custom_fusion.1 = f32[1536,768]{1,0:T(8,128)} fusion(s32[768]{0:T(1024)S(1)} %fusion.26, f32[]{:T(128)} %constant.55.clone.1, f32[768,768]{1,0:T(8,128)S(1)} %copy-done, f32[768]{0:T(1024)S(1)} %add_rsqrt_fusion), kind=kCustom, calls=%fused_computation.17 | custom fusion | flops 589824 | bytes 7081988 | tf_op jit(solution)/shard_map/scatter | solution.py:77
  23.1 9.6 %all-to-all-start.1 = ((f32[32,48,768]{2,1,0:T(8,128)}), f32[32,48,768]{2,1,0:T(8,128)}, u32[]{:S(2)}, u32[]{:S(2)}) async-start(f32[32,48,768]{2,1,0:T(8,128)} %bitcast.46), calls=%async_computation.1 | async-start | bytes 9437184 | tf_op jit(solution)/shard_map/all_to_all | solution.py:80
  37.1 55.2 %all-to-all-done.1 = f32[32,48,768]{2,1,0:T(8,128)} async-done(((f32[32,48,768]{2,1,0:T(8,128)}), f32[32,48,768]{2,1,0:T(8,128)}, u32[]{:S(2)}, u32[]{:S(2)}) %all-to-all-start.1) | async-done | bytes 4718624 | tf_op jit(solution)/shard_map/all_to_all | solution.py:80
  96.4 9.8 %all-to-all-start = ((s32[32,1,48]{2,1,0:T(1,128)}), s32[32,1,48]{2,1,0:T(1,128)S(1)}, u32[]{:S(2)}, u32[]{:S(2)}) async-start(s32[32,1,48]{2,1,0:T(1,128)} %all_to_all.17), calls=%async_computation | async-start | bytes 32768 | tf_op jit(solution)/shard_map/all_to_all | solution.py:87
  106.2 11.3 %reduce-scatter.2.cloned.1.call-done = f32[16,768]{1,0:T(8,128)} async-done(((f32[512,768]{1,0:T(8,128)}), f32[16,768]{1,0:T(8,128)}) %reduce-scatter.2.cloned.1.call-update) | async-done | bytes 49168 | tf_op jit(solution)/shard_map/reduce_scatter | solution.py:117
  126.8 10.4 %all-gather = s32[4,1,1536]{2,1,0:T(1,128)S(1)} all-gather(s32[1,1,1536]{2,1,0:T(1,128)S(1)} %reshape.149), channel_id=1, replica_groups=mesh['grp'=4,'own'=32] {'grp'}, dimensions={0}, use_global_device_ids=true | all-gather | bytes 30720 | tf_op jit(solution)/shard_map/all_gather | solution.py:97
  137.4 132.1 %all-gather.3.cloned.1.call-done = f32[6144,768]{1,0:T(8,128)} async-done(((f32[1536,768]{1,0:T(8,128)}), f32[6144,768]{1,0:T(8,128)}) %all-gather.3.cloned.1.call-update) | async-done | bytes 18874384 | tf_op jit(solution)/shard_map/all_gather | solution.py:96
  269.5 131.6 %while.14 = (s32[]{:T(128)}, f32[1536]{0:T(1024)S(1)}, s32[32,48]{1,0:T(8,128)}, s32[12,512]{1,0:T(8,128)S(1)}, f32[12,512,768]{2,1,0:T(8,128)}, /*index=5*/f32[...) while((s32[]{:T(128)}, f32[1536]{0:T(1024)S(1)}, s32[32,48]{1,0:T(8,128)}, ...), condition=%wide.wide.region_9.10_spmd.clone, body=%wide.wide.region_7.9_spmd.clone.sunk | while | flops 7252478976 | bytes 6338155 | solution.py:56
  269.5 10.9 %fusion.38 = f32[1536]{0:T(1024)S(1)} fusion(f32[1536,768]{1,0:T(8,128)} %get-tuple-element.205, f32[12,512,768]{2,1,0:T(8,128)} %get-tuple-element.204, s32[]{:T(128)} %get-tuple-element.191, pred[1536]{0:T(1024)(128)(4,1)S(1)} %broadcast_compare_fusion.3, s32[512]{0:T(512)S(1)} %bitcast.50, s32[1536]{0:T(1024)S(1)} %get-tuple-element.206), kind=kOutput, calls=%fused_computation.11.clone.clone.1 | convolution fusion | flops 7252474368 | bytes 6307840 | tf_op jit(solution)/shard_map/while/body/eval_jaxpr/id,jd->ij/dot_general | solution.py:33
  280.5 10.9 %fusion.38 = f32[1536]{0:T(1024)S(1)} fusion(f32[1536,768]{1,0:T(8,128)} %get-tuple-element.205, f32[12,512,768]{2,1,0:T(8,128)} %get-tuple-element.204, s32[]{:T(128)} %get-tuple-element.191, pred[1536]{0:T(1024)(128)(4,1)S(1)} %broadcast_compare_fusion.3, s32[512]{0:T(512)S(1)} %bitcast.50, s32[1536]{0:T(1024)S(1)} %get-tuple-element.206), kind=kOutput, calls=%fused_computation.11.clone.clone.1 | convolution fusion | flops 7252474368 | bytes 6307840 | tf_op jit(solution)/shard_map/while/body/eval_jaxpr/id,jd->ij/dot_general | solution.py:33
  291.5 10.9 %fusion.38 = f32[1536]{0:T(1024)S(1)} fusion(f32[1536,768]{1,0:T(8,128)} %get-tuple-element.205, f32[12,512,768]{2,1,0:T(8,128)} %get-tuple-element.204, s32[]{:T(128)} %get-tuple-element.191, pred[1536]{0:T(1024)(128)(4,1)S(1)} %broadcast_compare_fusion.3, s32[512]{0:T(512)S(1)} %bitcast.50, s32[1536]{0:T(1024)S(1)} %get-tuple-element.206), kind=kOutput, calls=%fused_computation.11.clone.clone.1 | convolution fusion | flops 7252474368 | bytes 6307840 | tf_op jit(solution)/shard_map/while/body/eval_jaxpr/id,jd->ij/dot_general | solution.py:33
  302.4 10.9 %fusion.38 = f32[1536]{0:T(1024)S(1)} fusion(f32[1536,768]{1,0:T(8,128)} %get-tuple-element.205, f32[12,512,768]{2,1,0:T(8,128)} %get-tuple-element.204, s32[]{:T(128)} %get-tuple-element.191, pred[1536]{0:T(1024)(128)(4,1)S(1)} %broadcast_compare_fusion.3, s32[512]{0:T(512)S(1)} %bitcast.50, s32[1536]{0:T(1024)S(1)} %get-tuple-element.206), kind=kOutput, calls=%fused_computation.11.clone.clone.1 | convolution fusion | flops 7252474368 | bytes 6307840 | tf_op jit(solution)/shard_map/while/body/eval_jaxpr/id,jd->ij/dot_general | solution.py:33
  313.4 10.9 %fusion.38 = f32[1536]{0:T(1024)S(1)} fusion(f32[1536,768]{1,0:T(8,128)} %get-tuple-element.205, f32[12,512,768]{2,1,0:T(8,128)} %get-tuple-element.204, s32[]{:T(128)} %get-tuple-element.191, pred[1536]{0:T(1024)(128)(4,1)S(1)} %broadcast_compare_fusion.3, s32[512]{0:T(512)S(1)} %bitcast.50, s32[1536]{0:T(1024)S(1)} %get-tuple-element.206), kind=kOutput, calls=%fused_computation.11.clone.clone.1 | convolution fusion | flops 7252474368 | bytes 6307840 | tf_op jit(solution)/shard_map/while/body/eval_jaxpr/id,jd->ij/dot_general | solution.py:33
  324.4 10.9 %fusion.38 = f32[1536]{0:T(1024)S(1)} fusion(f32[1536,768]{1,0:T(8,128)} %get-tuple-element.205, f32[12,512,768]{2,1,0:T(8,128)} %get-tuple-element.204, s32[]{:T(128)} %get-tuple-element.191, pred[1536]{0:T(1024)(128)(4,1)S(1)} %broadcast_compare_fusion.3, s32[512]{0:T(512)S(1)} %bitcast.50, s32[1536]{0:T(1024)S(1)} %get-tuple-element.206), kind=kOutput, calls=%fused_computation.11.clone.clone.1 | convolution fusion | flops 7252474368 | bytes 6307840 | tf_op jit(solution)/shard_map/while/body/eval_jaxpr/id,jd->ij/dot_general | solution.py:33
  335.3 10.9 %fusion.38 = f32[1536]{0:T(1024)S(1)} fusion(f32[1536,768]{1,0:T(8,128)} %get-tuple-element.205, f32[12,512,768]{2,1,0:T(8,128)} %get-tuple-element.204, s32[]{:T(128)} %get-tuple-element.191, pred[1536]{0:T(1024)(128)(4,1)S(1)} %broadcast_compare_fusion.3, s32[512]{0:T(512)S(1)} %bitcast.50, s32[1536]{0:T(1024)S(1)} %get-tuple-element.206), kind=kOutput, calls=%fused_computation.11.clone.clone.1 | convolution fusion | flops 7252474368 | bytes 6307840 | tf_op jit(solution)/shard_map/while/body/eval_jaxpr/id,jd->ij/dot_general | solution.py:33
  346.3 10.9 %fusion.38 = f32[1536]{0:T(1024)S(1)} fusion(f32[1536,768]{1,0:T(8,128)} %get-tuple-element.205, f32[12,512,768]{2,1,0:T(8,128)} %get-tuple-element.204, s32[]{:T(128)} %get-tuple-element.191, pred[1536]{0:T(1024)(128)(4,1)S(1)} %broadcast_compare_fusion.3, s32[512]{0:T(512)S(1)} %bitcast.50, s32[1536]{0:T(1024)S(1)} %get-tuple-element.206), kind=kOutput, calls=%fused_computation.11.clone.clone.1 | convolution fusion | flops 7252474368 | bytes 6307840 | tf_op jit(solution)/shard_map/while/body/eval_jaxpr/id,jd->ij/dot_general | solution.py:33
  357.3 10.9 %fusion.38 = f32[1536]{0:T(1024)S(1)} fusion(f32[1536,768]{1,0:T(8,128)} %get-tuple-element.205, f32[12,512,768]{2,1,0:T(8,128)} %get-tuple-element.204, s32[]{:T(128)} %get-tuple-element.191, pred[1536]{0:T(1024)(128)(4,1)S(1)} %broadcast_compare_fusion.3, s32[512]{0:T(512)S(1)} %bitcast.50, s32[1536]{0:T(1024)S(1)} %get-tuple-element.206), kind=kOutput, calls=%fused_computation.11.clone.clone.1 | convolution fusion | flops 7252474368 | bytes 6307840 | tf_op jit(solution)/shard_map/while/body/eval_jaxpr/id,jd->ij/dot_general | solution.py:33
  368.2 10.9 %fusion.38 = f32[1536]{0:T(1024)S(1)} fusion(f32[1536,768]{1,0:T(8,128)} %get-tuple-element.205, f32[12,512,768]{2,1,0:T(8,128)} %get-tuple-element.204, s32[]{:T(128)} %get-tuple-element.191, pred[1536]{0:T(1024)(128)(4,1)S(1)} %broadcast_compare_fusion.3, s32[512]{0:T(512)S(1)} %bitcast.50, s32[1536]{0:T(1024)S(1)} %get-tuple-element.206), kind=kOutput, calls=%fused_computation.11.clone.clone.1 | convolution fusion | flops 7252474368 | bytes 6307840 | tf_op jit(solution)/shard_map/while/body/eval_jaxpr/id,jd->ij/dot_general | solution.py:33
  379.2 10.9 %fusion.38 = f32[1536]{0:T(1024)S(1)} fusion(f32[1536,768]{1,0:T(8,128)} %get-tuple-element.205, f32[12,512,768]{2,1,0:T(8,128)} %get-tuple-element.204, s32[]{:T(128)} %get-tuple-element.191, pred[1536]{0:T(1024)(128)(4,1)S(1)} %broadcast_compare_fusion.3, s32[512]{0:T(512)S(1)} %bitcast.50, s32[1536]{0:T(1024)S(1)} %get-tuple-element.206), kind=kOutput, calls=%fused_computation.11.clone.clone.1 | convolution fusion | flops 7252474368 | bytes 6307840 | tf_op jit(solution)/shard_map/while/body/eval_jaxpr/id,jd->ij/dot_general | solution.py:33
  390.2 10.9 %fusion.38 = f32[1536]{0:T(1024)S(1)} fusion(f32[1536,768]{1,0:T(8,128)} %get-tuple-element.205, f32[12,512,768]{2,1,0:T(8,128)} %get-tuple-element.204, s32[]{:T(128)} %get-tuple-element.191, pred[1536]{0:T(1024)(128)(4,1)S(1)} %broadcast_compare_fusion.3, s32[512]{0:T(512)S(1)} %bitcast.50, s32[1536]{0:T(1024)S(1)} %get-tuple-element.206), kind=kOutput, calls=%fused_computation.11.clone.clone.1 | convolution fusion | flops 7252474368 | bytes 6307840 | tf_op jit(solution)/shard_map/while/body/eval_jaxpr/id,jd->ij/dot_general | solution.py:33
  401.8 7.8 %all-to-all-start.2 = ((f32[32,1,48]{2,1,0:T(1,128)}), f32[32,1,48]{2,1,0:T(1,128)S(1)}, u32[]{:S(2)}, u32[]{:S(2)}) async-start(f32[32,1,48]{2,1,0:T(1,128)} %all_to_all.21), calls=%async_computation.2 | async-start | bytes 32768 | tf_op jit(solution)/shard_map/all_to_all | solution.py:99
  410.3 6.2 %all-to-all-done.2 = f32[32,1,48]{2,1,0:T(1,128)S(1)} async-done(((f32[32,1,48]{2,1,0:T(1,128)}), f32[32,1,48]{2,1,0:T(1,128)S(1)}, u32[]{:S(2)}, u32[]{:S(2)}) %all-to-all-start.2) | async-done | bytes 6176 | tf_op jit(solution)/shard_map/all_to_all | solution.py:99
  417.8 4.5 %gather_fusion = f32[768]{0:T(1024)S(1)} fusion(f32[1536]{0:T(1024)S(1)} %reshape.115, s32[1024]{0:T(1024)S(1)} %pad_clamp_fusion), kind=kCustom, calls=%fused_computation | custom fusion | bytes 9216 | tf_op jit(solution)/shard_map/gather | solution.py:102
  422.3 3.9 scatter_custom_fusion.2
  (89 shorter events, 26.2 us)
Async XLA Ops:
  8.0 5.3 %copy-start = (f32[768,768]{1,0:T(8,128)S(1)}, f32[768,768]{1,0:T(8,128)}, u32[]{:S(2)}) copy-start(f32[768,768]{1,0:T(8,128)} %param.6) | copy-start | bytes 7077892
  23.1 9.7 %copy-start.2 = (s32[512]{0:T(512)S(1)}, s32[512]{0:T(512)}, u32[]{:S(2)}) copy-start(s32[512]{0:T(512)} %param.8) | copy-start | bytes 6148
  23.1 10.1 %copy-start.3 = (s32[768]{0:T(1024)S(1)}, s32[768]{0:T(1024)}, u32[]{:S(2)}) copy-start(s32[768]{0:T(1024)} %param.7) | copy-start | bytes 9220
  23.1 69.2 %all-to-all-start.1 = ((f32[32,48,768]{2,1,0:T(8,128)}), f32[32,48,768]{2,1,0:T(8,128)}, u32[]{:S(2)}, u32[]{:S(2)}) async-start(f32[32,48,768]{2,1,0:T(8,128)} %bitcast.46), calls=%async_computation.1 | async-start | bytes 9437184 | tf_op jit(solution)/shard_map/all_to_all | solution.py:80
  32.7 84.8 %reduce-scatter.2.cloned.1.call-start = ((), (), s32[]{:S(2)}) async-start(), calls=%async_computation.5 | async-start | bytes 1622016 | tf_op jit(solution)/shard_map/reduce_scatter | solution.py:117
  37.0 232.5 %all-gather.3.cloned.1.call-start = ((), (), s32[]{:S(2)}) async-start(), calls=%async_computation.4 | async-start | bytes 23592960 | tf_op jit(solution)/shard_map/all_gather | solution.py:96
  92.3 26.4 %copy-start.4 = (s32[768]{0:T(1024)S(1)}, s32[768]{0:T(1024)}, u32[]{:S(2)}) copy-start(s32[768]{0:T(1024)} %param.9) | copy-start | bytes 9220
  96.4 29.1 %all-to-all-start = ((s32[32,1,48]{2,1,0:T(1,128)}), s32[32,1,48]{2,1,0:T(1,128)S(1)}, u32[]{:S(2)}, u32[]{:S(2)}) async-start(s32[32,1,48]{2,1,0:T(1,128)} %all_to_all.17), calls=%async_computation | async-start | bytes 32768 | tf_op jit(solution)/shard_map/all_to_all | solution.py:87
  117.5 4.6 %collective-permute-start = (f32[16,768]{1,0:T(8,128)}, f32[16,768]{1,0:T(8,128)S(1)}, u32[]{:S(2)}, u32[]{:S(2)}) collective-permute-start(f32[16,768]{1,0:T(8,128)} %reduce-scatter.2.cloned.1.call-done), channel_id=1, source_target_pairs={{0,32},{32,0},{64,96},{96,64},{1,33},{33,1},{65,97},{97,65},{2,34}... | collective-permute-start | bytes 147464 | tf_op jit(solution)/shard_map/ppermute | solution.py:14
  122.8 14.5 %collective-permute-start.1 = (f32[16,768]{1,0:T(8,128)S(1)}, f32[16,768]{1,0:T(8,128)S(1)}, u32[]{:S(2)}, u32[]{:S(2)}) collective-permute-start(f32[16,768]{1,0:T(8,128)S(1)} %add.95), channel_id=1, source_target_pairs={{0,64},{32,96},{64,0},{96,32},{1,65},{33,97},{65,1},{97,33},{2,66}... | collective-permute-start | bytes 147464 | tf_op jit(solution)/shard_map/ppermute | solution.py:14
  125.5 143.9 %copy-start.1 = (s32[32,1,48]{2,1,0:T(1,128)}, s32[32,1,48]{2,1,0:T(1,128)S(1)}, u32[]{:S(2)}) copy-start(s32[32,1,48]{2,1,0:T(1,128)S(1)} %all-to-all-done) | copy-start | bytes 18436
  401.8 14.7 %all-to-all-start.2 = ((f32[32,1,48]{2,1,0:T(1,128)}), f32[32,1,48]{2,1,0:T(1,128)S(1)}, u32[]{:S(2)}, u32[]{:S(2)}) async-start(f32[32,1,48]{2,1,0:T(1,128)} %all_to_all.21), calls=%async_computation.2 | async-start | bytes 32768 | tf_op jit(solution)/shard_map/all_to_all | solution.py:99
Sparse Core Ops, SparseCore 0:
  37.1 80.2 reduce-scatter.1
Sparse Core Ops, SparseCore 1:
  92.4 177.0 all-gather.2
